TPU v7x, 256 devices: a whole 4x4x8 slice. The times are simulated.
256 devices in a mesh: tm: 4 (over z_hi, core), height: 16 (over x, y), width: 4 (over z_lo).
Axes of the slice: x: 4, y: 4, z: 8 (z_hi: 2, z_lo: 4; z = z_hi * 4 + z_lo), core: 2. Of those that a mesh axis runs over, the one named last changes fastest.
Arguments:
- frames: bfloat16 [8, 64, 128, 384], P('tm', 'height', 'width'), may hold values from -6 to 6
- cache_in: bfloat16 [2, 64, 128, 384], P(None, 'height', 'width'), may hold values from -6 to 6
- kernel: bfloat16 [384, 3, 3, 3, 384], replicated, may hold values from -0.0625 to 0.0625
- conv_bias: float32 [384], replicated, may hold values from -3 to 3
- cotangent: bfloat16 [8, 64, 128, 384], P('tm', 'height', 'width'), may hold values from -6 to 6
Outputs:
- decoded: bfloat16 [8, 64, 128, 384], P('tm', 'height', 'width')
- frame_grad: bfloat16 [8, 64, 128, 384], P('tm', 'height', 'width')
- cache_grad: bfloat16 [8, 64, 128, 384], P('tm', 'height', 'width')
- kernel_grad: float32 [384, 3, 3, 3, 384], P('height')
All inputs are finite; a program needn't handle non-finite values.
Results may differ from a plain program's by a relative error of at most 0.0053.
Values may be sent and summed in bfloat16 or wider, within the bound.
No kernel may reach another device: no remote copies, remote signals or barrier semaphores. Data moves between devices by JAX's collectives and lax.ppermute only.
A program may use at most 256 MiB of HBM per device.

v0:
```python
import jax
import jax.numpy as jnp
from jax import lax
from jax.sharding import PartitionSpec as P


def shifted(value, axis, by):
    length = lax.axis_size(axis)
    pairs = [(i, i + by) for i in range(length) if 0 <= i + by < length]
    return lax.ppermute(value, axis, pairs)


def with_halo(value, sides, width):
    for axis, dim in sides:
        size, length = (lax.axis_size(axis), value.shape[dim])
        up = [(i, (i + 1) % size) for i in range(size - 1)]
        down = [(j, i) for i, j in up]
        last = lax.slice_in_dim(value, length - width, length, axis=dim)
        initial = lax.slice_in_dim(value, 0, width, axis=dim)
        before = lax.ppermute(last, axis, up)
        after = lax.ppermute(initial, axis, down)
        value = jnp.concatenate([before, value, after], axis=dim)
    return value


def tap_block(padded, tap_t, tap_h, tap_w, depth_count, row_count, col_count):
    block = padded[
        tap_t : tap_t + depth_count, tap_h : tap_h + row_count, tap_w : tap_w + col_count
    ]
    return block.reshape(-1, block.shape[-1])


def body(frames, cache_in, kernel, conv_bias, cotangent):
    frame_count, row_count, col_count, channels = frames.shape
    is_first = lax.axis_index("tm") == 0
    earlier = shifted(frames, "tm", 1)
    earlier = jnp.where(is_first, cache_in, earlier)
    stacked = jnp.concatenate([earlier, frames], 0)
    extended = with_halo(stacked, (("height", 1), ("width", 2)), 1)
    pre_act = jnp.zeros((frame_count * row_count * col_count, channels), jnp.float32) + conv_bias
    for tap_t in range(3):
        for tap_h in range(3):
            for tap_w in range(3):
                block = tap_block(extended, tap_t, tap_h, tap_w, frame_count, row_count, col_count)
                pre_act = pre_act + lax.dot_general(
                    block,
                    kernel[:, tap_t, tap_h, tap_w, :],
                    (((1,), (1,)), ((), ())),
                    preferred_element_type=jnp.float32,
                )
    sigma = jax.nn.sigmoid(pre_act)
    decoded = (pre_act * sigma).astype(jnp.bfloat16).reshape(frames.shape)
    scaled = (
        cotangent.reshape(-1, channels).astype(jnp.float32)
        * sigma
        * (1.0 + pre_act * (1.0 - sigma))
    ).astype(jnp.bfloat16)
    grad_rimmed = with_halo(scaled.reshape(frames.shape), (("height", 1), ("width", 2)), 1)
    partial_value = jnp.zeros((frame_count + 2, row_count, col_count, channels), jnp.float32)
    for tap_t in range(3):
        contrib = jnp.zeros((frame_count * row_count * col_count, channels), jnp.float32)
        for tap_h in range(3):
            for tap_w in range(3):
                block = grad_rimmed[
                    :, 2 - tap_h : 2 - tap_h + row_count, 2 - tap_w : 2 - tap_w + col_count
                ].reshape(-1, channels)
                contrib = contrib + jnp.dot(
                    block, kernel[:, tap_t, tap_h, tap_w, :], preferred_element_type=jnp.float32
                )
        partial_value = partial_value.at[tap_t : tap_t + frame_count].add(
            contrib.reshape(frame_count, row_count, col_count, channels)
        )
    cache_grad = partial_value[:2].astype(jnp.bfloat16)
    carried = shifted(cache_grad, "tm", -1)
    frame_grad = (
        partial_value[2:]
        .at[frame_count - 2 :]
        .add(carried.astype(jnp.float32))
        .astype(jnp.bfloat16)
    )
    pieces = []
    for tap_t in range(3):
        for tap_h in range(3):
            for tap_w in range(3):
                block = tap_block(extended, tap_t, tap_h, tap_w, frame_count, row_count, col_count)
                pieces.append(
                    lax.dot_general(
                        scaled, block, (((0,), (0,)), ((), ())), preferred_element_type=jnp.float32
                    )
                )
    owned = lax.psum_scatter(
        jnp.stack(pieces, 1).reshape(
            channels // lax.axis_size("height") * lax.axis_size("height"), 3, 3, 3, channels
        ),
        "height",
        scatter_dimension=0,
        tiled=True,
    )
    kernel_grad = lax.psum(owned, ("tm", "width"))
    return (decoded, frame_grad, cache_grad, kernel_grad)


def solution(mesh):
    in_specs = (
        P("tm", "height", "width", None),
        P(None, "height", "width", None),
        P(),
        P(),
        P("tm", "height", "width", None),
    )
    out_specs = (
        P("tm", "height", "width", None),
        P("tm", "height", "width", None),
        P("tm", "height", "width", None),
        P("height", None, None, None, None),
    )
    return jax.shard_map(body, mesh=mesh, in_specs=in_specs, out_specs=out_specs, check_vma=False)
```

profile of v0, /device:TPU:1, one launch (start us, length us, event | category | flops | bytes accessed | tf_op | source)
XLA Modules:
  0.0 323.4 jit_solution(16105572426888722058)
XLA Ops:
  7.2 10.2 %collective-permute-start = (bf16[2,4,32,384]{3,2,1,0:T(8,128)(2,1)}, bf16[2,4,32,384]{3,2,1,0:T(8,128)(2,1)S(1)}, u32[]{:S(2)}, u32[]{:S(2)}) collective-permute-start(bf16[2,4,32,384]{3,2,1,0:T(8,128)(2,1)} %param.15), channel_id=1, source_target_pairs={{0,64},{64,128},{128,192},{1,65},{65,129},{129,193},{2,66},{66,130... | collective-permute-start | bytes 589832 | tf_op jit(solution)/shard_map/ppermute | solution.py:10
  17.4 2.9 collective-permute-done
  21.2 3.2 collective-permute-start.1
  24.4 1.3 collective-permute-start.2
  26.7 3.1 collective-permute-done.2
  30.7 4.8 %collective-permute-start.3 = (bf16[4,6,1,384]{3,2,1,0:T(2,128)(2,1)S(1)}, bf16[4,6,1,384]{3,2,1,0:T(2,128)(2,1)S(1)}, u32[]{:S(2)}, u32[]{:S(2)}) collective-permute-start(bf16[4,6,1,384]{3,2,1,0:T(2,128)(2,1)S(1)} %get-tuple-element.80), channel_id=1, source_target_pairs={{0,1},{1,2},{2,3},{4,5},{5,6},{6,7},{8,9},{9,10},{10,11},{12,13},{... | collective-permute-start | bytes 55304 | tf_op jit(solution)/shard_map/ppermute | solution.py:20
  35.5 1.3 collective-permute-start.4
  36.8 1.1 pad_maximum_fusion.1
  38.1 2.1 collective-permute-done.4
  40.2 1.4 maximum_maximum_fusion
  65.4 1.2 fusion.13
  66.6 1.2 fusion.12
  74.4 1.2 fusion.5
  81.3 3.5 %collective-permute-start.5 = (bf16[2,1,32,384]{3,2,1,0:T(8,128)(2,1)S(1)}, bf16[2,1,32,384]{3,2,1,0:T(8,128)(2,1)S(1)}, u32[]{:S(2)}, u32[]{:S(2)}) collective-permute-start(bf16[2,1,32,384]{3,2,1,0:T(8,128)(2,1)S(1)} %get-tuple-element.106), channel_id=1, source_target_pairs={{0,4},{4,8},{8,12},{12,16},{16,20},{20,24},{24,28},{28,32},{32,36}... | collective-permute-start | bytes 147464 | tf_op jit(solution)/shard_map/ppermute | solution.py:20
  84.7 1.3 collective-permute-start.6
  86.1 3.5 %collective-permute-done.6 = bf16[2,1,32,384]{3,2,1,0:T(8,128)(2,1)S(1)} collective-permute-done((bf16[2,1,32,384]{3,2,1,0:T(8,128)(2,1)S(1)}, bf16[2,1,32,384]{3,2,1,0:T(8,128)(2,1)S(1)}, u32[]{:S(2)}, u32[]{:S(2)}) %collective-permute-start.6) | collective-permute-done | bytes 49184 | tf_op jit(solution)/shard_map/ppermute | solution.py:21
  89.6 1.3 collective-permute-start.7
  90.9 4.2 %collective-permute-start.8 = (bf16[2,6,1,384]{3,2,1,0:T(2,128)(2,1)S(1)}, bf16[2,6,1,384]{3,2,1,0:T(2,128)(2,1)S(1)}, u32[]{:S(2)}, u32[]{:S(2)}) collective-permute-start(bf16[2,6,1,384]{3,2,1,0:T(2,128)(2,1)S(1)} %get-tuple-element.103), channel_id=1, source_target_pairs={{0,1},{1,2},{2,3},{4,5},{5,6},{6,7},{8,9},{9,10},{10,11},{12,13},{... | collective-permute-start | bytes 27656 | tf_op jit(solution)/shard_map/ppermute | solution.py:20
  95.1 1.2 fusion.70
  96.4 1.2 fusion.91
  97.6 1.2 fusion.50
  99.2 1.5 fusion.75
  100.7 1.3 convolution_add_fusion.20
  102.0 1.2 convolution_add_fusion.19
  103.3 1.2 convolution_add_fusion.18
  104.5 1.2 convolution_add_fusion.17
  105.8 1.2 convolution_add_fusion.16
  110.0 1.9 collective-permute-start.9
  113.9 87.3 %reduce-scatter.2.cloned.1.call-done = f32[24,3,3,3,384]{4,0,3,2,1:T(8,128)} async-done(((f32[384,3,3,3,384]{4,0,3,2,1:T(8,128)}), f32[24,3,3,3,384]{4,0,3,2,1:T(8,128)}) %reduce-scatter.2.cloned.1.call-update) | async-done | bytes 995344 | tf_op jit(solution)/shard_map/reduce_scatter | solution.py:91
  201.2 1.2 fusion.30
  203.2 111.2 %all-reduce.3.cloned.1.call-done = f32[24,3,3,3,384]{4,0,3,2,1:T(8,128)} async-done(((f32[24,3,3,3,384]{4,0,3,2,1:T(8,128)}), f32[24,3,3,3,384]{4,0,3,2,1:T(8,128)}) %all-reduce.3.cloned.1.call-update) | async-done | bytes 995344 | tf_op jit(solution)/shard_map/psum | solution.py:99
  314.3 2.2 copy.37
  (112 shorter events, 44.7 us)
Async XLA Ops:
  7.2 194.0 %reduce-scatter.2.cloned.1.call-start = ((), (), s32[]{:S(2)}) async-start(), calls=%async_computation.1 | async-start | bytes 16920576 | tf_op jit(solution)/shard_map/reduce_scatter | solution.py:91
  7.2 13.1 %collective-permute-start = (bf16[2,4,32,384]{3,2,1,0:T(8,128)(2,1)}, bf16[2,4,32,384]{3,2,1,0:T(8,128)(2,1)S(1)}, u32[]{:S(2)}, u32[]{:S(2)}) collective-permute-start(bf16[2,4,32,384]{3,2,1,0:T(8,128)(2,1)} %param.15), channel_id=1, source_target_pairs={{0,64},{64,128},{128,192},{1,65},{65,129},{129,193},{2,66},{66,130... | collective-permute-start | bytes 589832 | tf_op jit(solution)/shard_map/ppermute | solution.py:10
  17.4 24.6 %slice-start = ((s8[7962624]{0:T(1024)(128)(4,1)}), s8[4194304]{0:T(1024)(128)(4,1)S(1)}, s32[]{:S(2)}) async-start(s8[7962624]{0:T(1024)(128)(4,1)} %bitcast.401), calls=%async_computation.3 | async-start | bytes 8388608
  20.4 22.0 %copy-start.2 = (f32[384]{0:T(512)S(1)}, f32[384]{0:T(512)}, u32[]{:S(2)}) copy-start(f32[384]{0:T(512)} %param.18) | copy-start | bytes 4612
  21.2 5.4 %collective-permute-start.1 = (bf16[4,1,32,384]{3,2,1,0:T(8,128)(2,1)S(1)}, bf16[4,1,32,384]{3,2,1,0:T(8,128)(2,1)S(1)}, u32[]{:S(2)}, u32[]{:S(2)}) collective-permute-start(bf16[4,1,32,384]{3,2,1,0:T(8,128)(2,1)S(1)} %get-tuple-element.92), channel_id=1, source_target_pairs={{0,4},{4,8},{8,12},{12,16},{16,20},{20,24},{24,28},{28,32},{32,36}... | collective-permute-start | bytes 294920 | tf_op jit(solution)/shard_map/ppermute | solution.py:20
  24.4 5.4 %collective-permute-start.2 = (bf16[4,1,32,384]{3,2,1,0:T(8,128)(2,1)S(1)}, bf16[4,1,32,384]{3,2,1,0:T(8,128)(2,1)S(1)}, u32[]{:S(2)}, u32[]{:S(2)}) collective-permute-start(bf16[4,1,32,384]{3,2,1,0:T(8,128)(2,1)S(1)} %get-tuple-element.93), channel_id=1, source_target_pairs={{4,0},{8,4},{12,8},{16,12},{20,16},{24,20},{28,24},{32,28},{36,32}... | collective-permute-start | bytes 294920 | tf_op jit(solution)/shard_map/ppermute | solution.py:21
  30.7 7.4 %collective-permute-start.3 = (bf16[4,6,1,384]{3,2,1,0:T(2,128)(2,1)S(1)}, bf16[4,6,1,384]{3,2,1,0:T(2,128)(2,1)S(1)}, u32[]{:S(2)}, u32[]{:S(2)}) collective-permute-start(bf16[4,6,1,384]{3,2,1,0:T(2,128)(2,1)S(1)} %get-tuple-element.80), channel_id=1, source_target_pairs={{0,1},{1,2},{2,3},{4,5},{5,6},{6,7},{8,9},{9,10},{10,11},{12,13},{... | collective-permute-start | bytes 55304 | tf_op jit(solution)/shard_map/ppermute | solution.py:20
  35.5 4.7 %collective-permute-start.4 = (bf16[4,6,1,384]{3,2,1,0:T(2,128)(2,1)S(1)}, bf16[4,6,1,384]{3,2,1,0:T(2,128)(2,1)S(1)}, u32[]{:S(2)}, u32[]{:S(2)}) collective-permute-start(bf16[4,6,1,384]{3,2,1,0:T(2,128)(2,1)S(1)} %get-tuple-element.81), channel_id=1, source_target_pairs={{1,0},{2,1},{3,2},{5,4},{6,5},{7,6},{9,8},{10,9},{11,10},{13,12},{... | collective-permute-start | bytes 55304 | tf_op jit(solution)/shard_map/ppermute | solution.py:21
  38.1 4.0 %slice-start.1 = ((s8[7962624]{0:T(1024)(128)(4,1)}), s8[3768320]{0:T(1024)(128)(4,1)S(1)}, s32[]{:S(2)}) async-start(s8[7962624]{0:T(1024)(128)(4,1)} %bitcast.401), calls=%async_computation.4 | async-start | bytes 7536640
  45.0 3.6 %copy-start = (bf16[2,4,32,384]{3,2,1,0:T(8,128)(2,1)S(1)}, bf16[2,4,32,384]{3,2,1,0:T(8,128)(2,1)}, u32[]{:S(2)}) copy-start(bf16[2,4,32,384]{3,2,1,0:T(8,128)(2,1)} %param.15) | copy-start | bytes 589828
  46.2 3.6 %copy-start.3 = (bf16[2,4,32,384]{3,2,1,0:T(8,128)(2,1)S(1)}, bf16[2,4,32,384]{3,2,1,0:T(8,128)(2,1)}, u32[]{:S(2)}) copy-start(bf16[2,4,32,384]{3,2,1,0:T(8,128)(2,1)} %param.19) | copy-start | bytes 589828
  81.2 233.1 %all-reduce.3.cloned.1.call-start = ((), (), s32[]{:S(2)}) async-start(), calls=%async_computation.2 | async-start | bytes 1990656 | tf_op jit(solution)/shard_map/psum | solution.py:99
  81.2 25.8 %slice-start.2 = ((s8[7962624]{0:T(1024)(128)(4,1)}), s8[3768320]{0:T(1024)(128)(4,1)S(1)}, s32[]{:S(2)}) async-start(s8[7962624]{0:T(1024)(128)(4,1)} %bitcast.403), calls=%async_computation.5 | async-start | bytes 7536640
  81.3 4.8 %collective-permute-start.5 = (bf16[2,1,32,384]{3,2,1,0:T(8,128)(2,1)S(1)}, bf16[2,1,32,384]{3,2,1,0:T(8,128)(2,1)S(1)}, u32[]{:S(2)}, u32[]{:S(2)}) collective-permute-start(bf16[2,1,32,384]{3,2,1,0:T(8,128)(2,1)S(1)} %get-tuple-element.106), channel_id=1, source_target_pairs={{0,4},{4,8},{8,12},{12,16},{16,20},{20,24},{24,28},{28,32},{32,36}... | collective-permute-start | bytes 147464 | tf_op jit(solution)/shard_map/ppermute | solution.py:20
  84.7 4.8 %collective-permute-start.6 = (bf16[2,1,32,384]{3,2,1,0:T(8,128)(2,1)S(1)}, bf16[2,1,32,384]{3,2,1,0:T(8,128)(2,1)S(1)}, u32[]{:S(2)}, u32[]{:S(2)}) collective-permute-start(bf16[2,1,32,384]{3,2,1,0:T(8,128)(2,1)S(1)} %get-tuple-element.107), channel_id=1, source_target_pairs={{4,0},{8,4},{12,8},{16,12},{20,16},{24,20},{28,24},{32,28},{36,32}... | collective-permute-start | bytes 147464 | tf_op jit(solution)/shard_map/ppermute | solution.py:21
  89.6 9.2 %collective-permute-start.7 = (bf16[2,6,1,384]{3,2,1,0:T(2,128)(2,1)S(1)}, bf16[2,6,1,384]{3,2,1,0:T(2,128)(2,1)S(1)}, u32[]{:S(2)}, u32[]{:S(2)}) collective-permute-start(bf16[2,6,1,384]{3,2,1,0:T(2,128)(2,1)S(1)} %get-tuple-element.102), channel_id=1, source_target_pairs={{1,0},{2,1},{3,2},{5,4},{6,5},{7,6},{9,8},{10,9},{11,10},{13,12},{... | collective-permute-start | bytes 27656 | tf_op jit(solution)/shard_map/ppermute | solution.py:21
  90.9 7.9 %collective-permute-start.8 = (bf16[2,6,1,384]{3,2,1,0:T(2,128)(2,1)S(1)}, bf16[2,6,1,384]{3,2,1,0:T(2,128)(2,1)S(1)}, u32[]{:S(2)}, u32[]{:S(2)}) collective-permute-start(bf16[2,6,1,384]{3,2,1,0:T(2,128)(2,1)S(1)} %get-tuple-element.103), channel_id=1, source_target_pairs={{0,1},{1,2},{2,3},{4,5},{5,6},{6,7},{8,9},{9,10},{10,11},{12,13},{... | collective-permute-start | bytes 27656 | tf_op jit(solution)/shard_map/ppermute | solution.py:20
  99.1 7.9 %slice-start.3 = ((s8[7962624]{0:T(1024)(128)(4,1)}), s8[4194304]{0:T(1024)(128)(4,1)S(1)}, s32[]{:S(2)}) async-start(s8[7962624]{0:T(1024)(128)(4,1)} %bitcast.403), calls=%async_computation.6 | async-start | bytes 8388608
  110.0 206.6 %copy-start.1 = (bf16[2,4,32,384]{3,2,1,0:T(8,128)(2,1)}, bf16[2,4,32,384]{3,2,1,0:T(8,128)(2,1)S(1)}, u32[]{:S(2)}) copy-start(bf16[2,4,32,384]{3,2,1,0:T(8,128)(2,1)S(1)} %slice.745) | copy-start | bytes 589828
  110.0 92.4 %collective-permute-start.9 = (bf16[2,4,32,384]{3,2,1,0:T(8,128)(2,1)S(1)}, bf16[2,4,32,384]{3,2,1,0:T(8,128)(2,1)S(1)}, u32[]{:S(2)}, u32[]{:S(2)}) collective-permute-start(bf16[2,4,32,384]{3,2,1,0:T(8,128)(2,1)S(1)} %slice.745), channel_id=1, source_target_pairs={{64,0},{128,64},{192,128},{65,1},{129,65},{193,129},{66,2},{130,66... | collective-permute-start | bytes 589832 | tf_op jit(solution)/shard_map/ppermute | solution.py:10
Sparse Core Ops, SparseCore 0:
  81.3 119.7 reduce-scatter.1
  203.5 110.8 all-reduce.2
where the time goes:
time: 324 us; the launch traced here: 323 us
  waiting for transfers between devices  210 us (65%)
  matrix products  56 us (17%)
  starting transfers between devices  33 us (10%)
  between operations  14.8 us (5%)
  other arithmetic  6.37 us (2%)
    psum x1, waiting for transfers between devices, body(): kernel_grad = lax.psum(owned, ('tm', 'width'))  111 us
    reduce_scatter x1, waiting for transfers between devices, body(): lax.psum_scatter(jnp.stack(pieces, 1).reshape(channels // lax.axis_size('...  87.3 us
    dot_general x27, matrix products, body(): lax.dot_general(scaled, block, (((0,), (0,)), ((), ())), preferred_elemen...  30.3 us
    dot_general x27, matrix products, body(): jnp.dot(block, kernel[:, tap_t, tap_h, tap_w, :], preferred_element_type=...  17.2 us
    ppermute x4, starting transfers between devices, with_halo(): before = lax.ppermute(last, axis, up)  15.6 us
    ppermute x2, starting transfers between devices, shifted(): return lax.ppermute(value, axis, pairs)  12.1 us
    ppermute x4, waiting for transfers between devices, with_halo(): after = lax.ppermute(initial, axis, down)  8.73 us
    dot_general x27, matrix products, body(): lax.dot_general(block, kernel[:, tap_t, tap_h, tap_w, :], (((1,), (1,)),...  8.56 us
  transfers between devices with their start and end apart: 12, of which 6 were waited for; matrix products, arithmetic and copies ran while one was open for 6% of the time, Pallas kernels for 0%

commit v1 on v0

--- a/solution.py
+++ b/solution.py
@@ -96,7 +96,7 @@
         scatter_dimension=0,
         tiled=True,
     )
-    kernel_grad = lax.psum(owned, ("tm", "width"))
+    kernel_grad = lax.psum(lax.psum(owned, "width"), "tm")
     return (decoded, frame_grad, cache_grad, kernel_grad)
 
 

time: 324 us -> 347 us (1.071)
  matrix products: 56 us -> 72.3 us
  waiting for transfers between devices: 210 us -> 216 us
    dot_general x27, matrix products: 17.2 us -> 33.4 us  [body(): jnp.dot(block, kernel[:, tap_t, tap_h, tap_w, :], preferred_element_type=...]
    psum x1 -> x2, waiting for transfers between devices: 111 us -> 126 us  [body(): kernel_grad = lax.psum(lax.psum(owned, 'width'), 'tm')]
    reduce_scatter x1, waiting for transfers between devices: 87.3 us -> 78.8 us  [body(): lax.psum_scatter(jnp.stack(pieces, 1).reshape(channels // lax.axis_size('...]
  transfers between devices with their start and end apart: 12 -> 13, of which waited for: 6 -> 7; matrix products, arithmetic and copies ran while one was open for 6% -> 11% of each run, Pallas kernels for 0% -> 0%
where the time goes in v1:
time: 347 us; the launch traced here: 345 us
  waiting for transfers between devices  216 us (62%)
  matrix products  72.3 us (21%)
  starting transfers between devices  32.7 us (9%)
  between operations  14.5 us (4%)
  other arithmetic  6.35 us (2%)
    psum x2, waiting for transfers between devices, body(): kernel_grad = lax.psum(lax.psum(owned, 'width'), 'tm')  126 us
    reduce_scatter x1, waiting for transfers between devices, body(): lax.psum_scatter(jnp.stack(pieces, 1).reshape(channels // lax.axis_size('...  78.8 us
    dot_general x27, matrix products, body(): jnp.dot(block, kernel[:, tap_t, tap_h, tap_w, :], preferred_element_type=...  33.4 us
    dot_general x27, matrix products, body(): lax.dot_general(scaled, block, (((0,), (0,)), ((), ())), preferred_elemen...  30.3 us
    ppermute x4, starting transfers between devices, with_halo(): before = lax.ppermute(last, axis, up)  15.3 us
    ppermute x2, starting transfers between devices, shifted(): return lax.ppermute(value, axis, pairs)  12.1 us
    ppermute x4, waiting for transfers between devices, with_halo(): after = lax.ppermute(initial, axis, down)  8.73 us
    dot_general x27, matrix products, body(): lax.dot_general(block, kernel[:, tap_t, tap_h, tap_w, :], (((1,), (1,)),...  8.56 us
  transfers between devices with their start and end apart: 13, of which 7 were waited for; matrix products, arithmetic and copies ran while one was open for 11% of the time, Pallas kernels for 0%

profile of v1, /device:TPU:1, one launch (start us, length us, event | category | flops | bytes accessed | tf_op | source)
XLA Modules:
  0.0 345.3 jit_solution(11185927172986731955)
XLA Ops:
  7.2 10.2 %collective-permute-start = (bf16[2,4,32,384]{3,2,1,0:T(8,128)(2,1)}, bf16[2,4,32,384]{3,2,1,0:T(8,128)(2,1)S(1)}, u32[]{:S(2)}, u32[]{:S(2)}) collective-permute-start(bf16[2,4,32,384]{3,2,1,0:T(8,128)(2,1)} %param.15), channel_id=1, source_target_pairs={{0,64},{64,128},{128,192},{1,65},{65,129},{129,193},{2,66},{66,130... | collective-permute-start | bytes 589832 | tf_op jit(solution)/shard_map/ppermute | solution.py:10
  17.4 2.9 collective-permute-done
  21.2 3.2 collective-permute-start.1
  24.4 1.3 collective-permute-start.2
  26.7 3.1 collective-permute-done.2
  30.7 4.8 %collective-permute-start.3 = (bf16[4,6,1,384]{3,2,1,0:T(2,128)(2,1)S(1)}, bf16[4,6,1,384]{3,2,1,0:T(2,128)(2,1)S(1)}, u32[]{:S(2)}, u32[]{:S(2)}) collective-permute-start(bf16[4,6,1,384]{3,2,1,0:T(2,128)(2,1)S(1)} %get-tuple-element.80), channel_id=1, source_target_pairs={{0,1},{1,2},{2,3},{4,5},{5,6},{6,7},{8,9},{9,10},{10,11},{12,13},{... | collective-permute-start | bytes 55304 | tf_op jit(solution)/shard_map/ppermute | solution.py:20
  35.5 1.3 collective-permute-start.4
  38.1 2.1 collective-permute-done.4
  40.2 1.4 maximum_maximum_fusion
  81.3 3.2 collective-permute-start.5
  84.5 1.3 collective-permute-start.6
  85.8 3.5 %collective-permute-done.6 = bf16[2,1,32,384]{3,2,1,0:T(8,128)(2,1)S(1)} collective-permute-done((bf16[2,1,32,384]{3,2,1,0:T(8,128)(2,1)S(1)}, bf16[2,1,32,384]{3,2,1,0:T(8,128)(2,1)S(1)}, u32[]{:S(2)}, u32[]{:S(2)}) %collective-permute-start.6) | collective-permute-done | bytes 49184 | tf_op jit(solution)/shard_map/ppermute | solution.py:21
  89.4 1.3 collective-permute-start.7
  90.7 4.2 %collective-permute-start.8 = (bf16[2,6,1,384]{3,2,1,0:T(2,128)(2,1)S(1)}, bf16[2,6,1,384]{3,2,1,0:T(2,128)(2,1)S(1)}, u32[]{:S(2)}, u32[]{:S(2)}) collective-permute-start(bf16[2,6,1,384]{3,2,1,0:T(2,128)(2,1)S(1)} %get-tuple-element.103), channel_id=1, source_target_pairs={{0,1},{1,2},{2,3},{4,5},{5,6},{6,7},{8,9},{9,10},{10,11},{12,13},{... | collective-permute-start | bytes 27656 | tf_op jit(solution)/shard_map/ppermute | solution.py:20
  99.0 1.3 fusion.75
  100.3 1.2 convolution_add_fusion.20
  105.3 1.2 convolution_add_fusion.16
  106.5 1.2 convolution_add_fusion.15
  107.8 1.2 fusion.28
  110.3 1.2 convolution_add_fusion.13
  112.8 1.2 convolution_add_fusion.11
  115.3 1.2 convolution_add_fusion.9
  116.5 1.2 convolution_add_fusion.8
  117.8 1.3 fusion.29
  119.2 1.9 collective-permute-start.9
  121.1 1.2 convolution_add_fusion.6
  122.4 78.8 %reduce-scatter.2.cloned.1.call-done = f32[24,3,3,3,384]{4,0,3,2,1:T(8,128)} async-done(((f32[384,3,3,3,384]{4,0,3,2,1:T(8,128)}), f32[24,3,3,3,384]{4,0,3,2,1:T(8,128)}) %reduce-scatter.2.cloned.1.call-update) | async-done | bytes 995344 | tf_op jit(solution)/shard_map/reduce_scatter | solution.py:91
  205.0 1.2 convolution_add_fusion.2
  206.3 58.9 %all-reduce.4.cloned.1.call-done = f32[24,3,3,3,384]{4,0,3,2,1:T(8,128)} async-done(((f32[24,3,3,3,384]{4,0,3,2,1:T(8,128)}), f32[24,3,3,3,384]{4,0,3,2,1:T(8,128)}) %all-reduce.4.cloned.1.call-update) | async-done | bytes 995344 | tf_op jit(solution)/shard_map/psum | solution.py:99
  267.7 1.2 fusion.30
  269.7 66.9 %all-reduce.6.cloned.1.call-done = f32[24,3,3,3,384]{4,0,3,2,1:T(8,128)} async-done(((f32[24,3,3,3,384]{4,0,3,2,1:T(8,128)}), f32[24,3,3,3,384]{4,0,3,2,1:T(8,128)}) %all-reduce.6.cloned.1.call-update) | async-done | bytes 995344 | tf_op jit(solution)/shard_map/psum | solution.py:99
  336.6 2.2 copy.38
  (110 shorter events, 62.1 us)
Async XLA Ops:
  7.2 194.1 %reduce-scatter.2.cloned.1.call-start = ((), (), s32[]{:S(2)}) async-start(), calls=%async_computation.1 | async-start | bytes 16920576 | tf_op jit(solution)/shard_map/reduce_scatter | solution.py:91
  7.2 13.1 %collective-permute-start = (bf16[2,4,32,384]{3,2,1,0:T(8,128)(2,1)}, bf16[2,4,32,384]{3,2,1,0:T(8,128)(2,1)S(1)}, u32[]{:S(2)}, u32[]{:S(2)}) collective-permute-start(bf16[2,4,32,384]{3,2,1,0:T(8,128)(2,1)} %param.15), channel_id=1, source_target_pairs={{0,64},{64,128},{128,192},{1,65},{65,129},{129,193},{2,66},{66,130... | collective-permute-start | bytes 589832 | tf_op jit(solution)/shard_map/ppermute | solution.py:10
  17.4 24.6 %slice-start = ((s8[7962624]{0:T(1024)(128)(4,1)}), s8[4194304]{0:T(1024)(128)(4,1)S(1)}, s32[]{:S(2)}) async-start(s8[7962624]{0:T(1024)(128)(4,1)} %bitcast.401), calls=%async_computation.4 | async-start | bytes 8388608
  20.4 22.0 %copy-start.2 = (f32[384]{0:T(512)S(1)}, f32[384]{0:T(512)}, u32[]{:S(2)}) copy-start(f32[384]{0:T(512)} %param.18) | copy-start | bytes 4612
  21.2 5.4 %collective-permute-start.1 = (bf16[4,1,32,384]{3,2,1,0:T(8,128)(2,1)S(1)}, bf16[4,1,32,384]{3,2,1,0:T(8,128)(2,1)S(1)}, u32[]{:S(2)}, u32[]{:S(2)}) collective-permute-start(bf16[4,1,32,384]{3,2,1,0:T(8,128)(2,1)S(1)} %get-tuple-element.92), channel_id=1, source_target_pairs={{0,4},{4,8},{8,12},{12,16},{16,20},{20,24},{24,28},{28,32},{32,36}... | collective-permute-start | bytes 294920 | tf_op jit(solution)/shard_map/ppermute | solution.py:20
  24.4 5.4 %collective-permute-start.2 = (bf16[4,1,32,384]{3,2,1,0:T(8,128)(2,1)S(1)}, bf16[4,1,32,384]{3,2,1,0:T(8,128)(2,1)S(1)}, u32[]{:S(2)}, u32[]{:S(2)}) collective-permute-start(bf16[4,1,32,384]{3,2,1,0:T(8,128)(2,1)S(1)} %get-tuple-element.93), channel_id=1, source_target_pairs={{4,0},{8,4},{12,8},{16,12},{20,16},{24,20},{28,24},{32,28},{36,32}... | collective-permute-start | bytes 294920 | tf_op jit(solution)/shard_map/ppermute | solution.py:21
  30.7 7.4 %collective-permute-start.3 = (bf16[4,6,1,384]{3,2,1,0:T(2,128)(2,1)S(1)}, bf16[4,6,1,384]{3,2,1,0:T(2,128)(2,1)S(1)}, u32[]{:S(2)}, u32[]{:S(2)}) collective-permute-start(bf16[4,6,1,384]{3,2,1,0:T(2,128)(2,1)S(1)} %get-tuple-element.80), channel_id=1, source_target_pairs={{0,1},{1,2},{2,3},{4,5},{5,6},{6,7},{8,9},{9,10},{10,11},{12,13},{... | collective-permute-start | bytes 55304 | tf_op jit(solution)/shard_map/ppermute | solution.py:20
  35.5 4.7 %collective-permute-start.4 = (bf16[4,6,1,384]{3,2,1,0:T(2,128)(2,1)S(1)}, bf16[4,6,1,384]{3,2,1,0:T(2,128)(2,1)S(1)}, u32[]{:S(2)}, u32[]{:S(2)}) collective-permute-start(bf16[4,6,1,384]{3,2,1,0:T(2,128)(2,1)S(1)} %get-tuple-element.81), channel_id=1, source_target_pairs={{1,0},{2,1},{3,2},{5,4},{6,5},{7,6},{9,8},{10,9},{11,10},{13,12},{... | collective-permute-start | bytes 55304 | tf_op jit(solution)/shard_map/ppermute | solution.py:21
  38.1 4.0 %slice-start.1 = ((s8[7962624]{0:T(1024)(128)(4,1)}), s8[3768320]{0:T(1024)(128)(4,1)S(1)}, s32[]{:S(2)}) async-start(s8[7962624]{0:T(1024)(128)(4,1)} %bitcast.401), calls=%async_computation.5 | async-start | bytes 7536640
  45.0 3.6 %copy-start = (bf16[2,4,32,384]{3,2,1,0:T(8,128)(2,1)S(1)}, bf16[2,4,32,384]{3,2,1,0:T(8,128)(2,1)}, u32[]{:S(2)}) copy-start(bf16[2,4,32,384]{3,2,1,0:T(8,128)(2,1)} %param.15) | copy-start | bytes 589828
  46.2 3.6 %copy-start.3 = (bf16[2,4,32,384]{3,2,1,0:T(8,128)(2,1)S(1)}, bf16[2,4,32,384]{3,2,1,0:T(8,128)(2,1)}, u32[]{:S(2)}) copy-start(bf16[2,4,32,384]{3,2,1,0:T(8,128)(2,1)} %param.19) | copy-start | bytes 589828
  81.2 183.9 %all-reduce.4.cloned.1.call-start = ((), (), s32[]{:S(2)}) async-start(), calls=%async_computation.2 | async-start | bytes 1990656 | tf_op jit(solution)/shard_map/psum | solution.py:99
  81.3 4.5 %collective-permute-start.5 = (bf16[2,1,32,384]{3,2,1,0:T(8,128)(2,1)S(1)}, bf16[2,1,32,384]{3,2,1,0:T(8,128)(2,1)S(1)}, u32[]{:S(2)}, u32[]{:S(2)}) collective-permute-start(bf16[2,1,32,384]{3,2,1,0:T(8,128)(2,1)S(1)} %get-tuple-element.106), channel_id=1, source_target_pairs={{0,4},{4,8},{8,12},{12,16},{16,20},{20,24},{24,28},{28,32},{32,36}... | collective-permute-start | bytes 147464 | tf_op jit(solution)/shard_map/ppermute | solution.py:20
  84.5 4.8 %collective-permute-start.6 = (bf16[2,1,32,384]{3,2,1,0:T(8,128)(2,1)S(1)}, bf16[2,1,32,384]{3,2,1,0:T(8,128)(2,1)S(1)}, u32[]{:S(2)}, u32[]{:S(2)}) collective-permute-start(bf16[2,1,32,384]{3,2,1,0:T(8,128)(2,1)S(1)} %get-tuple-element.107), channel_id=1, source_target_pairs={{4,0},{8,4},{12,8},{16,12},{20,16},{24,20},{28,24},{32,28},{36,32}... | collective-permute-start | bytes 147464 | tf_op jit(solution)/shard_map/ppermute | solution.py:21
  89.4 9.2 %collective-permute-start.7 = (bf16[2,6,1,384]{3,2,1,0:T(2,128)(2,1)S(1)}, bf16[2,6,1,384]{3,2,1,0:T(2,128)(2,1)S(1)}, u32[]{:S(2)}, u32[]{:S(2)}) collective-permute-start(bf16[2,6,1,384]{3,2,1,0:T(2,128)(2,1)S(1)} %get-tuple-element.102), channel_id=1, source_target_pairs={{1,0},{2,1},{3,2},{5,4},{6,5},{7,6},{9,8},{10,9},{11,10},{13,12},{... | collective-permute-start | bytes 27656 | tf_op jit(solution)/shard_map/ppermute | solution.py:21
  90.7 7.9 %collective-permute-start.8 = (bf16[2,6,1,384]{3,2,1,0:T(2,128)(2,1)S(1)}, bf16[2,6,1,384]{3,2,1,0:T(2,128)(2,1)S(1)}, u32[]{:S(2)}, u32[]{:S(2)}) collective-permute-start(bf16[2,6,1,384]{3,2,1,0:T(2,128)(2,1)S(1)} %get-tuple-element.103), channel_id=1, source_target_pairs={{0,1},{1,2},{2,3},{4,5},{5,6},{6,7},{8,9},{9,10},{10,11},{12,13},{... | collective-permute-start | bytes 27656 | tf_op jit(solution)/shard_map/ppermute | solution.py:20
  119.2 219.6 %copy-start.1 = (bf16[2,4,32,384]{3,2,1,0:T(8,128)(2,1)}, bf16[2,4,32,384]{3,2,1,0:T(8,128)(2,1)S(1)}, u32[]{:S(2)}) copy-start(bf16[2,4,32,384]{3,2,1,0:T(8,128)(2,1)S(1)} %slice.745) | copy-start | bytes 589828
  119.2 149.7 %collective-permute-start.9 = (bf16[2,4,32,384]{3,2,1,0:T(8,128)(2,1)S(1)}, bf16[2,4,32,384]{3,2,1,0:T(8,128)(2,1)S(1)}, u32[]{:S(2)}, u32[]{:S(2)}) collective-permute-start(bf16[2,4,32,384]{3,2,1,0:T(8,128)(2,1)S(1)} %slice.745), channel_id=1, source_target_pairs={{64,0},{128,64},{192,128},{65,1},{129,65},{193,129},{66,2},{130,66... | collective-permute-start | bytes 589832 | tf_op jit(solution)/shard_map/ppermute | solution.py:10
  201.3 135.3 %all-reduce.6.cloned.1.call-start = ((), (), s32[]{:S(2)}) async-start(), calls=%async_computation.3 | async-start | bytes 1990656 | tf_op jit(solution)/shard_map/psum | solution.py:99
Sparse Core Ops, SparseCore 0:
  81.4 119.8 reduce-scatter.1
  203.9 61.1 all-reduce.3
  267.9 68.6 all-reduce.5
